TPU v7x, 32 devices: a whole 2x2x4 slice. The times are simulated.
32 devices in a mesh: dp: 8 (over z, core), chan: 4 (over y, x).
Axes of the slice: x: 2, y: 2, z: 4, core: 2. Of those that a mesh axis runs over, the one named last changes fastest.
Arguments:
- images: bfloat16 [16, 16, 16, 2816], P('dp', None, None, 'chan'), may hold values from -6 to 6
- kernel: float32 [7, 7, 2816], P(None, None, 'chan'), may hold values from -0.875 to 0.875
- layernorm_gain: float32 [2816], P('chan'), may hold values from 0.25 to 1.75
- layernorm_bias: float32 [2816], P('chan'), may hold values from -3 to 3
- w_expand: bfloat16 [2816, 11264], P('dp', 'chan'), may hold values from -0.109375 to 0.109375
- w_reduce: bfloat16 [11264, 2816], P('chan', 'dp'), may hold values from -0.0546875 to 0.0546875
- layer_scale: float32 [2816], P('chan'), may hold values from 0.25 to 1
- cotangent: bfloat16 [16, 16, 16, 2816], P('dp', None, None, 'chan'), may hold values from -6 to 6
Outputs:
- output: bfloat16 [16, 16, 16, 2816], P('dp', None, None, 'chan')
- grad_images: bfloat16 [16, 16, 16, 2816], P('dp', None, None, 'chan')
- grad_kernel: float32 [7, 7, 2816], P(None, None, 'chan')
- gain_gradient: float32 [2816], P('chan')
- grad_bias: float32 [2816], P('chan')
- grad_expand: float32 [2816, 11264], P('dp', 'chan')
- grad_reduce: float32 [11264, 2816], P('chan', 'dp')
- grad_scale: float32 [2816], P('chan')
All inputs are finite; a program needn't handle non-finite values.
Results may differ from a plain program's by a relative error of at most 0.025.
Values may be sent and summed in bfloat16 or wider, within the bound.
A program may use at most 128 MiB of HBM per device.

v0:
```python
import math
import jax
import jax.numpy as jnp
from jax import lax
from jax.sharding import PartitionSpec as P

eps = 1e-06


def depthwise(field, kern):
    height = field.shape[1]
    breadth = field.shape[2]
    padded = jnp.pad(field, ((0, 0), (3, 3), (3, 3), (0, 0)))
    total = jnp.zeros(field.shape, jnp.float32)
    for i in range(7):
        for j in range(7):
            total = total + padded[:, i : i + height, j : j + breadth, :] * kern[i, j]
    return total


def normal_cdf(value):
    return 0.5 * (1.0 + jax.scipy.special.erf(value / math.sqrt(2.0)))


def swap_pairs(shift, n):
    return [(i, i ^ shift) for i in range(n)]


def chan_gather(block):
    n = lax.axis_size("chan")
    me = lax.axis_index("chan")
    width = block.shape[1]
    whole = jnp.zeros((block.shape[0], n * width), block.dtype)
    parts = [block] + [lax.ppermute(block, "chan", swap_pairs(k, n)) for k in range(1, n)]
    for k in range(n):
        whole = lax.dynamic_update_slice(whole, parts[k], (0, (me ^ k) * width))
    return whole


def chan_scatter(partial):
    n = lax.axis_size("chan")
    me = lax.axis_index("chan")
    width = partial.shape[1] // n
    total = lax.dynamic_slice_in_dim(partial, me * width, width, 1).astype(jnp.float32)
    for k in range(1, n):
        mine = lax.dynamic_slice_in_dim(partial, (me ^ k) * width, width, 1)
        total = total + lax.ppermute(mine, "chan", swap_pairs(k, n)).astype(jnp.float32)
    return total


def dp_scatter(partial):
    return lax.psum_scatter(partial, "dp", scatter_dimension=0, tiled=True)


def dp_total(value):
    n = lax.axis_size("dp")
    shift = 1
    while shift < n:
        value = value + lax.ppermute(value, "dp", swap_pairs(shift, n))
        shift *= 2
    return value


def body(
    images, kernel, layernorm_gain, layernorm_bias, w_expand, w_reduce, layer_scale, cotangent
):
    shape_in = images.shape
    height = shape_in[1]
    breadth = shape_in[2]
    positions = shape_in[0] * height * breadth
    local_chan = shape_in[3]
    image_width = local_chan * lax.axis_size("chan")
    xf = images.astype(jnp.float32)
    conv = depthwise(xf, kernel).reshape(positions, local_chan)
    mean_val = lax.psum(jnp.sum(conv, axis=1), "chan")[:, None] / image_width
    centred_rows = conv - mean_val
    var = lax.psum(jnp.sum(centred_rows * centred_rows, axis=1), "chan")[:, None] / image_width
    inverse_deviation = lax.rsqrt(var + eps)
    standardized_input = centred_rows * inverse_deviation
    normed_output = (standardized_input * layernorm_gain + layernorm_bias).astype(jnp.bfloat16)
    normed_all = chan_gather(normed_output)
    expand_all = lax.all_gather(w_expand, "dp", axis=0, tiled=True)
    pre = jnp.dot(normed_all, expand_all, preferred_element_type=jnp.float32)
    hidden = (pre * normal_cdf(pre)).astype(jnp.bfloat16)
    dyf = cotangent.astype(jnp.float32).reshape(positions, local_chan)
    dbranch = (dyf * layer_scale).astype(jnp.bfloat16)
    dbranch_all = chan_gather(dbranch)
    reduce_part = lax.dot_general(
        dbranch_all, hidden, (((0,), (0,)), ((), ())), preferred_element_type=jnp.float32
    ).astype(jnp.bfloat16)
    reduce_all = lax.all_gather(w_reduce, "dp", axis=1, tiled=True)
    reduce_part, reduce_all = lax.optimization_barrier((reduce_part, reduce_all))
    grad_reduce = dp_scatter(reduce_part).astype(jnp.float32).T
    dhidden = lax.dot_general(
        dbranch_all, reduce_all, (((1,), (1,)), ((), ())), preferred_element_type=jnp.float32
    )
    slope = normal_cdf(pre) + pre * jnp.exp(-0.5 * pre * pre) / math.sqrt(2.0 * math.pi)
    dpre = (dhidden * slope).astype(jnp.bfloat16)
    expand_part = lax.dot_general(
        normed_all, dpre, (((0,), (0,)), ((), ())), preferred_element_type=jnp.float32
    ).astype(jnp.bfloat16)
    expand_part, dpre, hidden, reduce_all = lax.optimization_barrier(
        (expand_part, dpre, hidden, reduce_all)
    )
    grad_expand = dp_scatter(expand_part).astype(jnp.float32)
    partial_normed = lax.dot_general(
        dpre, expand_all, (((1,), (1,)), ((), ())), preferred_element_type=jnp.float32
    )
    normed_grad = chan_scatter(partial_normed.astype(jnp.bfloat16))
    partial_branch = jnp.dot(hidden, reduce_all, preferred_element_type=jnp.float32)
    branch = chan_scatter(partial_branch.astype(jnp.bfloat16))
    xr = xf.reshape(positions, local_chan)
    output = (xr + layer_scale * branch).astype(jnp.bfloat16).reshape(shape_in)
    scale_part = jnp.sum(dyf * branch, axis=0)
    gain_partial = jnp.sum(normed_grad * standardized_input, axis=0)
    bias_part = jnp.sum(normed_grad, axis=0)
    standardized_grad = normed_grad * layernorm_gain
    first_half, second_half = lax.psum(
        (
            jnp.sum(standardized_grad, axis=1),
            jnp.sum(standardized_grad * standardized_input, axis=1),
        ),
        "chan",
    )
    conv_output_grad = inverse_deviation * (
        standardized_grad
        - first_half[:, None] / image_width
        - standardized_input * (second_half[:, None] / image_width)
    )
    conv_output_grad = conv_output_grad.reshape(shape_in)
    padded = jnp.pad(xf, ((0, 0), (3, 3), (3, 3), (0, 0)))
    dpad = jnp.pad(conv_output_grad, ((0, 0), (3, 3), (3, 3), (0, 0)))
    back = cotangent.astype(jnp.float32)
    kern_rows = []
    for i in range(7):
        tap_row = []
        for j in range(7):
            tap_row.append(
                jnp.sum(
                    padded[:, i : i + height, j : j + breadth, :] * conv_output_grad, axis=(0, 1, 2)
                )
            )
            back = back + dpad[:, 6 - i : 6 - i + height, 6 - j : 6 - j + breadth, :] * kernel[i, j]
        kern_rows.append(jnp.stack(tap_row))
    kernel_part = jnp.stack(kern_rows)
    grad_images = back.astype(jnp.bfloat16)
    small = dp_total(
        jnp.concatenate(
            [
                kernel_part.reshape(-1, local_chan),
                gain_partial[None],
                bias_part[None],
                scale_part[None],
            ]
        )
    )
    taps = kernel_part.shape[0] * kernel_part.shape[1]
    grad_kernel = small[:taps].reshape(kernel_part.shape)
    gain_gradient, grad_bias, grad_scale = (small[taps], small[taps + 1], small[taps + 2])
    return (
        output,
        grad_images,
        grad_kernel,
        gain_gradient,
        grad_bias,
        grad_expand,
        grad_reduce,
        grad_scale,
    )


def solution(mesh):
    in_specs = (
        P("dp", None, None, "chan"),
        P(None, None, "chan"),
        P("chan"),
        P("chan"),
        P("dp", "chan"),
        P("chan", "dp"),
        P("chan"),
        P("dp", None, None, "chan"),
    )
    out_specs = (
        P("dp", None, None, "chan"),
        P("dp", None, None, "chan"),
        P(None, None, "chan"),
        P("chan"),
        P("chan"),
        P("dp", "chan"),
        P("chan", "dp"),
        P("chan"),
    )
    return jax.shard_map(body, mesh=mesh, in_specs=in_specs, out_specs=out_specs, check_vma=False)
```

profile of v0, /device:TPU:0, one launch (start us, length us, event | category | flops | bytes accessed | tf_op | source)
XLA Modules:
  0.0 632.4 jit_solution(10809469362754886029)
XLA Ops:
  10.0 12.3 %fusion.108 = (f32[2,16,16]{2,1,0:T(8,128)S(1)}, f32[2,16,16,704]{3,2,1,0:T(8,128)S(1)}) fusion(f32[704]{0:T(1024)S(1)} %get-tuple-element.123, f32[704]{0:T(1024)S(1)} %get-tuple-element.124, f32[704]{0:T(1024)S(1)} %get-tuple-element.77, f32[704]{0:T(1024)S(1)} %get-tuple-element.78, f32[704]{0:T(1024)S(1)} %get-tuple-element.79, ...), kind=kLoop, calls=%fused_computation.344 | loop fusion | flops 35323392 | bytes 3023616 | tf_op jit(solution)/shard_map/reduce_sum | solution.py:75
  22.4 11.3 %psum.28 = f32[512]{0:T(512)S(1)} all-reduce(f32[512]{0:T(512)S(1)} %reduce_sum.509), channel_id=1, replica_groups=mesh['dp'=8,'chan'=4] {'chan'}, use_global_device_ids=true, to_apply=%region_1.2 | all-reduce | flops 512 | bytes 4096 | tf_op jit(solution)/shard_map/psum | solution.py:75
  34.2 7.9 %psum.29 = f32[512]{0:T(512)S(1)} all-reduce(f32[512]{0:T(512)S(1)} %reduce_sum.511), channel_id=1, replica_groups=mesh['dp'=8,'chan'=4] {'chan'}, use_global_device_ids=true, to_apply=%region_3.4 | all-reduce | flops 512 | bytes 4096 | tf_op jit(solution)/shard_map/psum | solution.py:77
  43.4 2.3 copy.16
  45.6 1.5 collective-permute-start
  47.1 2.1 fusion.104
  49.2 2.3 copy.22
  52.7 1.5 collective-permute-start.4
  54.2 1.5 collective-permute-start.2
  55.7 9.3 %collective-permute-done = bf16[512,704]{0,1:T(8,128)(2,1)} collective-permute-done((bf16[512,704]{0,1:T(8,128)(2,1)}, bf16[512,704]{0,1:T(8,128)(2,1)}, u32[]{:S(2)}, u32[]{:S(2)}) %collective-permute-start) | collective-permute-done | bytes 720928 | tf_op jit(solution)/shard_map/ppermute | solution.py:34
  65.0 1.5 collective-permute-start.5
  66.5 1.8 broadcast.39.clone
  68.3 8.1 %dynamic_update_slice.24 = bf16[512,2816]{1,0:T(8,128)(2,1)} dynamic-update-slice(bf16[512,2816]{1,0:T(8,128)(2,1)} %broadcast.39.clone, bf16[512,704]{1,0:T(8,128)(2,1)} %add_convert_fusion, s32[]{:T(128)} %constant.11.clone.1, s32[]{:T(128)S(6)} %select_n.8) | dynamic-update-slice | bytes 1441796 | tf_op jit(solution)/shard_map/dynamic_update_slice | solution.py:36
  76.4 1.8 broadcast.39.clone.1
  78.2 8.1 %dynamic_update_slice.28 = bf16[512,2816]{1,0:T(8,128)(2,1)} dynamic-update-slice(bf16[512,2816]{1,0:T(8,128)(2,1)} %broadcast.39.clone.1, bf16[512,704]{1,0:T(8,128)(2,1)} %fusion.104, s32[]{:T(128)} %constant.11.clone.1, s32[]{:T(128)S(6)} %select_n.8) | dynamic-update-slice | bytes 1441796 | tf_op jit(solution)/shard_map/dynamic_update_slice | solution.py:36
  86.3 2.3 copy.17
  88.6 9.0 %dynamic_update_slice.25 = bf16[512,2816]{1,0:T(8,128)(2,1)} dynamic-update-slice(bf16[512,2816]{1,0:T(8,128)(2,1)} %dynamic_update_slice.24, bf16[512,704]{1,0:T(8,128)(2,1)} %copy.17, s32[]{:T(128)} %constant.11.clone.1, s32[]{:T(128)S(6)} %select_n.9) | dynamic-update-slice | bytes 1441796 | tf_op jit(solution)/shard_map/dynamic_update_slice | solution.py:36
  97.6 2.3 copy.23
  99.8 9.0 %dynamic_update_slice.29 = bf16[512,2816]{1,0:T(8,128)(2,1)} dynamic-update-slice(bf16[512,2816]{1,0:T(8,128)(2,1)} %dynamic_update_slice.28, bf16[512,704]{1,0:T(8,128)(2,1)} %copy.23, s32[]{:T(128)} %constant.11.clone.1, s32[]{:T(128)S(6)} %select_n.9) | dynamic-update-slice | bytes 1441796 | tf_op jit(solution)/shard_map/dynamic_update_slice | solution.py:36
  108.8 2.3 copy.19
  111.1 8.1 %dynamic_update_slice.26 = bf16[512,2816]{1,0:T(8,128)(2,1)} dynamic-update-slice(bf16[512,2816]{1,0:T(8,128)(2,1)} %dynamic_update_slice.25, bf16[512,704]{1,0:T(8,128)(2,1)} %copy.19, s32[]{:T(128)} %constant.11.clone.1, s32[]{:T(128)S(6)} %select_n.10) | dynamic-update-slice | bytes 1441796 | tf_op jit(solution)/shard_map/dynamic_update_slice | solution.py:36
  119.2 2.3 copy.25
  121.4 8.1 %dynamic_update_slice.30 = bf16[512,2816]{1,0:T(8,128)(2,1)} dynamic-update-slice(bf16[512,2816]{1,0:T(8,128)(2,1)} %dynamic_update_slice.29, bf16[512,704]{1,0:T(8,128)(2,1)} %copy.25, s32[]{:T(128)} %constant.11.clone.1, s32[]{:T(128)S(6)} %select_n.10) | dynamic-update-slice | bytes 1441796 | tf_op jit(solution)/shard_map/dynamic_update_slice | solution.py:36
  129.5 2.3 copy.21
  131.8 8.3 %dynamic_update_slice.27 = bf16[512,2816]{1,0:T(8,128)(2,1)} dynamic-update-slice(bf16[512,2816]{1,0:T(8,128)(2,1)} %dynamic_update_slice.26, bf16[512,704]{1,0:T(8,128)(2,1)} %copy.21, s32[]{:T(128)} %constant.11.clone.1, s32[]{:T(128)S(6)} %select_n.11) | dynamic-update-slice | bytes 1441796 | tf_op jit(solution)/shard_map/dynamic_update_slice | solution.py:36
  140.1 2.3 copy.27
  142.4 8.3 %dynamic_update_slice.31 = bf16[512,2816]{1,0:T(8,128)(2,1)} dynamic-update-slice(bf16[512,2816]{1,0:T(8,128)(2,1)} %dynamic_update_slice.30, bf16[512,704]{1,0:T(8,128)(2,1)} %copy.27, s32[]{:T(128)} %constant.11.clone.1, s32[]{:T(128)S(6)} %select_n.11) | dynamic-update-slice | bytes 1441796 | tf_op jit(solution)/shard_map/dynamic_update_slice | solution.py:36
  150.8 5.2 all-gather.3.cloned.1.call-done
  156.0 15.2 %multiply_convert_fusion = (bf16[512,2816]{1,0:T(8,128)(2,1)S(1)}, f32[512,2816]{1,0:T(8,128)}) fusion(bf16[512,2816]{1,0:T(8,128)(2,1)} %dynamic_update_slice.27, bf16[2816,2816]{1,0:T(8,128)(2,1)} %all-gather.3.cloned.1.call-done), kind=kOutput, calls=%fused_computation.105 | convolution fusion | flops 8127381504 | bytes 27394048 | tf_op jit(solution)/shard_map/dot_general | solution.py:83
  171.2 1.6 copy-done.13
  172.8 12.4 %convolution_convert_fusion.1 = bf16[2816,2816]{1,0:T(8,128)(2,1)} fusion(bf16[512,2816]{1,0:T(8,128)(2,1)S(1)} %copy-done.7, bf16[512,2816]{1,0:T(8,128)(2,1)S(1)} %get-tuple-element.15), kind=kOutput, calls=%fused_computation.97 | convolution fusion | flops 8128102400 | bytes 21626880 | tf_op jit(solution)/shard_map/dot_general | solution.py:88
  185.1 114.3 %all-gather.5.cloned.1.call-done = bf16[2816,2816]{0,1:T(8,128)(2,1)} async-done(((bf16[2816,352]{0,1:T(8,128)(2,1)}), bf16[2816,2816]{0,1:T(8,128)(2,1)}) %all-gather.5.cloned.1.call-update) | async-done | bytes 15859728 | tf_op jit(solution)/shard_map/all_gather | solution.py:91
  299.6 15.3 %fusion.5 = bf16[512,2816]{1,0:T(8,128)(2,1)S(1)} fusion(f32[512,2816]{1,0:T(8,128)} %get-tuple-element.140, bf16[512,2816]{1,0:T(8,128)(2,1)} %dynamic_update_slice.31, bf16[2816,2816]{0,1:T(8,128)(2,1)} %all-gather.5.cloned.1.call-done), kind=kOutput, calls=%fused_computation.104 | convolution fusion | flops 8134590464 | bytes 27394048 | tf_op jit(solution)/shard_map/dot_general | solution.py:94
  314.9 1.5 copy-done.14
  316.4 11.9 %convolution_convert_fusion = bf16[2816,2816]{1,0:T(8,128)(2,1)} fusion(bf16[512,2816]{1,0:T(8,128)(2,1)S(1)} %copy-done.8, bf16[512,2816]{1,0:T(8,128)(2,1)S(1)} %fusion.5), kind=kOutput, calls=%fused_computation.96 | convolution fusion | flops 8128102400 | bytes 21626880 | tf_op jit(solution)/shard_map/dot_general | solution.py:99
  328.3 13.7 %convolution_convert_fusion.3 = bf16[512,2816]{1,0:T(8,128)(2,1)S(1)} fusion(bf16[512,2816]{1,0:T(8,128)(2,1)} %copy-done.13, bf16[2816,2816]{0,1:T(8,128)(2,1)} %all-gather.5.cloned.1.call-done), kind=kOutput, calls=%fused_computation.108 | convolution fusion | flops 8121614336 | bytes 21626880 | tf_op jit(solution)/shard_map/dot_general | solution.py:110
  342.1 2.8 constant_dynamic-slice_fusion.5
  344.8 2.3 copy.28
  347.1 2.3 copy.32
  349.4 2.3 copy.30
  355.1 13.5 %convolution_convert_fusion.2 = bf16[512,2816]{1,0:T(8,128)(2,1)S(1)} fusion(bf16[512,2816]{1,0:T(8,128)(2,1)} %copy-done.14, bf16[2816,2816]{1,0:T(8,128)(2,1)} %all-gather.3.cloned.1.call-done), kind=kOutput, calls=%fused_computation.107 | convolution fusion | flops 8121614336 | bytes 21626880 | tf_op jit(solution)/shard_map/dot_general | solution.py:106
  368.7 2.8 constant_dynamic-slice_fusion.2
  371.5 2.3 copy.34
  373.8 2.3 copy.36
  377.5 2.3 copy.38
  379.8 1.5 collective-permute-start.11
  381.3 5.0 collective-permute-done.7
  387.9 2.3 copy.31
  390.1 2.3 copy.33
  392.4 2.3 copy.29
  394.7 21.8 %collective-permute-done.10 = bf16[512,704]{0,1:T(8,128)(2,1)} collective-permute-done((bf16[512,704]{0,1:T(8,128)(2,1)}, bf16[512,704]{0,1:T(8,128)(2,1)}, u32[]{:S(2)}, u32[]{:S(2)}) %collective-permute-start.10) | collective-permute-done | bytes 720928 | tf_op jit(solution)/shard_map/ppermute | solution.py:47
  416.6 2.3 copy.37
  418.9 2.3 copy.39
  421.2 2.3 copy.35
  423.5 5.4 fusion.105
  429.0 10.0 %all-reduce.2 = (f32[512]{0:T(512)S(1)}, f32[512]{0:T(512)S(1)}) all-reduce(f32[512]{0:T(512)S(1)} %get-tuple-element.143, f32[512]{0:T(512)S(1)} %get-tuple-element.142), channel_id=1, replica_groups=mesh['dp'=8,'chan'=4] {'chan'}, use_global_device_ids=true, to_apply=%region_7.8 | all-reduce | flops 1024 | bytes 8192 | tf_op jit(solution)/shard_map/psum | solution.py:118
  438.9 6.5 %multiply_reduce_fusion.2 = (f32[704]{0:T(1024)S(1)}, f32[704]{0:T(1024)S(1)}, f32[704]{0:T(1024)S(1)}, f32[704]{0:T(1024)S(1)}, f32[704]{0:T(1024)S(1)}, /*inde...) fusion(f32[2,16,16,704]{3,2,1,0:T(8,128)S(1)} %convert_element_, ...), kind=kLoop, calls=%fused_computation.218 | loop fusion | flops 15486592 | bytes 5828864 | tf_op jit(solution)/shard_map/reduce_sum | solution.py:139
  445.7 4.1 multiply_reduce_fusion.1
  449.8 2.8 multiply_reduce_fusion.3
  455.2 6.7 %collective-permute-done.13 = f32[52,704]{1,0:T(8,128)S(1)} collective-permute-done((f32[52,704]{1,0:T(8,128)S(1)}, f32[52,704]{1,0:T(8,128)S(1)}, u32[]{:S(2)}, u32[]{:S(2)}) %collective-permute-start.13) | collective-permute-done | bytes 146464 | tf_op jit(solution)/shard_map/ppermute | solution.py:59
  462.9 12.3 %fusion.99 = bf16[2,16,16,704]{3,2,1,0:T(8,128)(2,1)} fusion(f32[2,16,16,704]{3,2,1,0:T(8,128)S(1)} %bitcast.104, bf16[2,16,16,704]{3,2,1,0:T(8,128)(2,1)S(1)} %copy-done.2, f32[704]{0:T(1024)S(1)} %get-tuple-element.123, f32[704]{0:T(1024)S(1)} %get-tuple-element.124, f32[704]{0:T(1024)S(1)} %get-tuple-element.77, f32[704]{0:T(1024)S(1)} %get-tuple-element.78, ...), kind=kLoop, calls=%fused_computation.203 | loop fusion | flops 36044800 | bytes 3021568 | tf_op jit(solution)/shard_map/convert_element_type | solution.py:146
  476.6 3.7 convert_bitcast_fusion
  480.3 141.6 %reduce-scatter.3.cloned.1.call-done = bf16[352,2816]{1,0:T(8,128)(2,1)} async-done(((bf16[2816,2816]{1,0:T(8,128)(2,1)}), bf16[352,2816]{1,0:T(8,128)(2,1)}) %reduce-scatter.3.cloned.1.call-update) | async-done | bytes 1982480 | tf_op jit(solution)/shard_map/reduce_scatter | solution.py:52
  621.9 3.7 convert_element_type.89
  (144 shorter events, 16.9 us)
Async XLA Ops:
  7.2 1.6 copy-start.3
  7.2 148.8 %all-gather.3.cloned.1.call-start = ((), (), s32[]{:S(2)}) async-start(), calls=%async_computation.2 | async-start | bytes 17842176 | tf_op jit(solution)/shard_map/all_gather | solution.py:82
  7.9 291.6 %all-gather.5.cloned.1.call-start = ((), (), s32[]{:S(2)}) async-start(), calls=%async_computation.3 | async-start | bytes 17842176 | tf_op jit(solution)/shard_map/all_gather | solution.py:91
  8.7 0.9 copy-start.9
  8.7 467.9 %reduce-scatter.5.cloned.1.call-start = ((), (), s32[]{:S(2)}) async-start(), calls=%async_computation.5 | async-start | bytes 17842176 | tf_op jit(solution)/shard_map/reduce_scatter | solution.py:52
  22.3 19.9 %copy-start.10 = (f32[704]{0:T(1024)S(1)}, f32[704]{0:T(1024)}, u32[]{:S(2)}) copy-start(f32[704]{0:T(1024)} %param.10) | copy-start | bytes 8452
  22.3 19.9 %copy-start.12 = (f32[704]{0:T(1024)S(1)}, f32[704]{0:T(1024)}, u32[]{:S(2)}) copy-start(f32[704]{0:T(1024)} %param.11) | copy-start | bytes 8452
  42.1 5.0 copy-start.11
  45.6 19.4 %collective-permute-start = (bf16[512,704]{0,1:T(8,128)(2,1)}, bf16[512,704]{0,1:T(8,128)(2,1)}, u32[]{:S(2)}, u32[]{:S(2)}) collective-permute-start(bf16[512,704]{0,1:T(8,128)(2,1)} %copy.16), channel_id=1, source_target_pairs={{0,1},{1,0},{2,3},{3,2},{4,5},{5,4},{6,7},{7,6},{8,9},{9,8},{10,11... | collective-permute-start | bytes 2162696 | tf_op jit(solution)/shard_map/ppermute | solution.py:34
  51.5 46.0 %collective-permute-start.3 = (bf16[512,704]{0,1:T(8,128)(2,1)}, bf16[512,704]{0,1:T(8,128)(2,1)}, u32[]{:S(2)}, u32[]{:S(2)}) collective-permute-start(bf16[512,704]{0,1:T(8,128)(2,1)} %copy.22), channel_id=1, source_target_pairs={{0,1},{1,0},{2,3},{3,2},{4,5},{5,4},{6,7},{7,6},{8,9},{9,8},{10,11... | collective-permute-start | bytes 2162696 | tf_op jit(solution)/shard_map/ppermute | solution.py:34
  52.2 56.7 %collective-permute-start.1 = (bf16[512,704]{0,1:T(8,128)(2,1)}, bf16[512,704]{0,1:T(8,128)(2,1)}, u32[]{:S(2)}, u32[]{:S(2)}) collective-permute-start(bf16[512,704]{0,1:T(8,128)(2,1)} %copy.16), channel_id=1, source_target_pairs={{0,2},{1,3},{2,0},{3,1},{4,6},{5,7},{6,4},{7,5},{8,10},{9,11},{10,... | collective-permute-start | bytes 2162696 | tf_op jit(solution)/shard_map/ppermute | solution.py:34
  52.7 66.5 %collective-permute-start.4 = (bf16[512,704]{0,1:T(8,128)(2,1)}, bf16[512,704]{0,1:T(8,128)(2,1)}, u32[]{:S(2)}, u32[]{:S(2)}) collective-permute-start(bf16[512,704]{0,1:T(8,128)(2,1)} %copy.22), channel_id=1, source_target_pairs={{0,2},{1,3},{2,0},{3,1},{4,6},{5,7},{6,4},{7,5},{8,10},{9,11},{10,... | collective-permute-start | bytes 2162696 | tf_op jit(solution)/shard_map/ppermute | solution.py:34
  54.2 75.3 %collective-permute-start.2 = (bf16[512,704]{0,1:T(8,128)(2,1)}, bf16[512,704]{0,1:T(8,128)(2,1)}, u32[]{:S(2)}, u32[]{:S(2)}) collective-permute-start(bf16[512,704]{0,1:T(8,128)(2,1)} %copy.16), channel_id=1, source_target_pairs={{0,3},{1,2},{2,1},{3,0},{4,7},{5,6},{6,5},{7,4},{8,11},{9,10},{10,... | collective-permute-start | bytes 2162696 | tf_op jit(solution)/shard_map/ppermute | solution.py:34
  65.0 75.1 %collective-permute-start.5 = (bf16[512,704]{0,1:T(8,128)(2,1)}, bf16[512,704]{0,1:T(8,128)(2,1)}, u32[]{:S(2)}, u32[]{:S(2)}) collective-permute-start(bf16[512,704]{0,1:T(8,128)(2,1)} %copy.22), channel_id=1, source_target_pairs={{0,3},{1,2},{2,1},{3,0},{4,7},{5,6},{6,5},{7,4},{8,11},{9,10},{10,... | collective-permute-start | bytes 2162696 | tf_op jit(solution)/shard_map/ppermute | solution.py:34
  156.0 16.8 %copy-start.7 = (bf16[512,2816]{1,0:T(8,128)(2,1)S(1)}, bf16[512,2816]{1,0:T(8,128)(2,1)}, u32[]{:S(2)}) copy-start(bf16[512,2816]{1,0:T(8,128)(2,1)} %dynamic_update_slice.31) | copy-start | bytes 8650756
  171.2 1.6 copy-start.13
  299.5 322.4 %reduce-scatter.3.cloned.1.call-start = ((), (), s32[]{:S(2)}) async-start(), calls=%async_computation.4 | async-start | bytes 17842176 | tf_op jit(solution)/shard_map/reduce_scatter | solution.py:52
  299.5 16.8 %copy-start.8 = (bf16[512,2816]{1,0:T(8,128)(2,1)S(1)}, bf16[512,2816]{1,0:T(8,128)(2,1)}, u32[]{:S(2)}) copy-start(bf16[512,2816]{1,0:T(8,128)(2,1)} %dynamic_update_slice.27) | copy-start | bytes 8650756
  314.8 1.5 copy-start.14
  342.1 2.8 copy-start.5
  351.7 34.7 %collective-permute-start.7 = (bf16[512,704]{0,1:T(8,128)(2,1)}, bf16[512,704]{0,1:T(8,128)(2,1)}, u32[]{:S(2)}, u32[]{:S(2)}) collective-permute-start(bf16[512,704]{0,1:T(8,128)(2,1)} %copy.30), channel_id=1, source_target_pairs={{0,2},{1,3},{2,0},{3,1},{4,6},{5,7},{6,4},{7,5},{8,10},{9,11},{10,... | collective-permute-start | bytes 2162696 | tf_op jit(solution)/shard_map/ppermute | solution.py:47
  353.1 37.0 %collective-permute-start.8 = (bf16[512,704]{0,1:T(8,128)(2,1)}, bf16[512,704]{0,1:T(8,128)(2,1)}, u32[]{:S(2)}, u32[]{:S(2)}) collective-permute-start(bf16[512,704]{0,1:T(8,128)(2,1)} %copy.32), channel_id=1, source_target_pairs={{0,3},{1,2},{2,1},{3,0},{4,7},{5,6},{6,5},{7,4},{8,11},{9,10},{10,... | collective-permute-start | bytes 2162696 | tf_op jit(solution)/shard_map/ppermute | solution.py:47
  354.6 37.8 %collective-permute-start.6 = (bf16[512,704]{0,1:T(8,128)(2,1)}, bf16[512,704]{0,1:T(8,128)(2,1)}, u32[]{:S(2)}, u32[]{:S(2)}) collective-permute-start(bf16[512,704]{0,1:T(8,128)(2,1)} %copy.28), channel_id=1, source_target_pairs={{0,1},{1,0},{2,3},{3,2},{4,5},{5,4},{6,7},{7,6},{8,9},{9,8},{10,11... | collective-permute-start | bytes 2162696 | tf_op jit(solution)/shard_map/ppermute | solution.py:47
  368.7 2.8 copy-start.6
  376.1 40.5 %collective-permute-start.10 = (bf16[512,704]{0,1:T(8,128)(2,1)}, bf16[512,704]{0,1:T(8,128)(2,1)}, u32[]{:S(2)}, u32[]{:S(2)}) collective-permute-start(bf16[512,704]{0,1:T(8,128)(2,1)} %copy.36), channel_id=1, source_target_pairs={{0,2},{1,3},{2,0},{3,1},{4,6},{5,7},{6,4},{7,5},{8,10},{9,11},{10,... | collective-permute-start | bytes 2162696 | tf_op jit(solution)/shard_map/ppermute | solution.py:47
  379.8 39.1 %collective-permute-start.11 = (bf16[512,704]{0,1:T(8,128)(2,1)}, bf16[512,704]{0,1:T(8,128)(2,1)}, u32[]{:S(2)}, u32[]{:S(2)}) collective-permute-start(bf16[512,704]{0,1:T(8,128)(2,1)} %copy.38), channel_id=1, source_target_pairs={{0,3},{1,2},{2,1},{3,0},{4,7},{5,6},{6,5},{7,4},{8,11},{9,10},{10,... | collective-permute-start | bytes 2162696 | tf_op jit(solution)/shard_map/ppermute | solution.py:47
  386.4 34.8 %collective-permute-start.9 = (bf16[512,704]{0,1:T(8,128)(2,1)}, bf16[512,704]{0,1:T(8,128)(2,1)}, u32[]{:S(2)}, u32[]{:S(2)}) collective-permute-start(bf16[512,704]{0,1:T(8,128)(2,1)} %copy.34), channel_id=1, source_target_pairs={{0,1},{1,0},{2,3},{3,2},{4,5},{5,4},{6,7},{7,6},{8,9},{9,8},{10,11... | collective-permute-start | bytes 2162696 | tf_op jit(solution)/shard_map/ppermute | solution.py:47
  445.4 4.4 copy-start
  445.7 4.2 copy-start.4
  452.7 10.3 %copy-start.1 = (f32[512,704]{1,0:T(8,128)S(1)}, f32[512,704]{1,0:T(8,128)}, u32[]{:S(2)}) copy-start(f32[512,704]{1,0:T(8,128)} %copy-done) | copy-start | bytes 4325380
  452.7 10.2 %copy-start.2 = (bf16[2,16,16,704]{3,2,1,0:T(8,128)(2,1)S(1)}, bf16[2,16,16,704]{3,2,1,0:T(8,128)(2,1)}, u32[]{:S(2)}) copy-start(bf16[2,16,16,704]{3,2,1,0:T(8,128)(2,1)} %param.15) | copy-start | bytes 2162692
  453.6 1.5 collective-permute-start.12
  455.1 6.7 %collective-permute-start.13 = (f32[52,704]{1,0:T(8,128)S(1)}, f32[52,704]{1,0:T(8,128)S(1)}, u32[]{:S(2)}, u32[]{:S(2)}) collective-permute-start(f32[52,704]{1,0:T(8,128)S(1)} %fusion.121), channel_id=1, source_target_pairs={{0,8},{4,12},{8,0},{12,4},{16,24},{20,28},{24,16},{28,20},{1,9},{5... | collective-permute-start | bytes 439304 | tf_op jit(solution)/shard_map/ppermute | solution.py:59
  461.8 13.4 %collective-permute-start.14 = (f32[52,704]{1,0:T(8,128)S(1)}, f32[52,704]{1,0:T(8,128)S(1)}, u32[]{:S(2)}, u32[]{:S(2)}) collective-permute-start(f32[52,704]{1,0:T(8,128)S(1)} %add.498), channel_id=1, source_target_pairs={{0,16},{4,20},{8,24},{12,28},{16,0},{20,4},{24,8},{28,12},{1,17},{... | collective-permute-start | bytes 439304 | tf_op jit(solution)/shard_map/ppermute | solution.py:59
Sparse Core Ops, SparseCore 0:
  9.7 146.2 all-gather.2
  157.6 141.8 all-gather.4
  301.8 157.9 reduce-scatter.4
  462.0 159.8 reduce-scatter.2
where the time goes:
time: 644 us; the launch traced here: 632 us
  waiting for transfers between devices  307 us (48%)
  local copies, waits for them, and re-layouts  128 us (20%)
  matrix products  82 us (13%)
  other arithmetic  54.9 us (9%)
  blocking collectives  29.2 us (5%)
  starting transfers between devices  16.5 us (3%)
  between operations  14.7 us (2%)
    reduce_scatter x2, waiting for transfers between devices, dp_scatter(): return lax.psum_scatter(partial, 'dp', scatter_dimension=0, tiled=True)  142 us
    all_gather x1, waiting for transfers between devices, body(): reduce_all = lax.all_gather(w_reduce, 'dp', axis=1, tiled=True)  114 us
    dynamic_update_slice x8, local copies, waits for them, and re-layouts, chan_gather(): whole = lax.dynamic_update_slice(whole, parts[k], (0, (me ^ k) * width))  67.1 us
    ppermute x6, waiting for transfers between devices, chan_scatter(): lax.ppermute(mine, 'chan', swap_pairs(k, n)).astype(jnp.float32)  26.9 us
    dynamic_slice x8, local copies, waits for them, and re-layouts, chan_scatter(): mine = lax.dynamic_slice_in_dim(partial, (me ^ k) * width, width, 1)  19.2 us
    dot_general x1, matrix products, body(): lax.dot_general(dbranch_all, reduce_all, (((1,), (1,)), ((), ())), prefer...  15.3 us
    dot_general x1, matrix products, body(): pre = jnp.dot(normed_all, expand_all, preferred_element_type=jnp.float32)  15.2 us
    ppermute x6, local copies, waits for them, and re-layouts, chan_scatter(): lax.ppermute(mine, 'chan', swap_pairs(k, n)).astype(jnp.float32)  13.8 us
  transfers between devices with their start and end apart: 19, of which 8 were waited for; matrix products, arithmetic and copies ran while one was open for 41% of the time, Pallas kernels for 0%

commit v1 on v0

--- a/solution.py
+++ b/solution.py
@@ -88,7 +88,19 @@
     reduce_part = lax.dot_general(
         dbranch_all, hidden, (((0,), (0,)), ((), ())), preferred_element_type=jnp.float32
     ).astype(jnp.bfloat16)
-    reduce_all = lax.all_gather(w_reduce, "dp", axis=1, tiled=True)
+    num = lax.axis_size("dp")
+    items = [(s, (s + 1) % num) for s in range(num)]
+    local_out, y2 = ([w_reduce], [w_reduce])
+    shelf = [(s, (s - 1) % num) for s in range(num)]
+    for _ in range(num // 2):
+        x_next = lax.ppermute(local_out[-1], "dp", perm=items)
+        local_out.append(x_next)
+    for _ in tuple(range((num - 1) // 2)):
+        reply = lax.ppermute(y2[-1], "dp", perm=shelf)
+        y2.append(reply)
+    val = jnp.concatenate([*local_out[::-1], *y2[1:]], axis=1)
+    block_last = lax.axis_index("dp")
+    reduce_all = jnp.roll(val, (block_last - num // 2) * w_reduce.shape[1], axis=1)
     reduce_part, reduce_all = lax.optimization_barrier((reduce_part, reduce_all))
     grad_reduce = dp_scatter(reduce_part).astype(jnp.float32).T
     dhidden = lax.dot_general(

time: 644 us -> 787 us (1.22)
  waiting for transfers between devices: 307 us -> 386 us
  starting transfers between devices: 16.5 us -> 77.7 us
    ppermute x0 -> x7, waiting for transfers between devices: none -> 169 us  [the longest x4 158 us: body(): x_next = lax.ppermute(local_out[-1], 'dp', perm=items)]
    all_gather x1 -> x0, waiting for transfers between devices: 114 us -> none  [body(): reduce_all = lax.all_gather(w_reduce, 'dp', axis=1, tiled=True)]
    ppermute x0 -> x7, starting transfers between devices: none -> 37.2 us  [the longest x4 25.6 us: body(): x_next = lax.ppermute(local_out[-1], 'dp', perm=items)]
    ppermute x3, starting transfers between devices: 1.25 us -> 24.8 us  [dp_total(): value = value + lax.ppermute(value, 'dp', swap_pairs(shift, n))]
    unnamed x36 -> x215, local copies, waits for them, and re-layouts: 3.88 us -> 27.3 us
    reduce_scatter x2, waiting for transfers between devices: 142 us -> 157 us  [dp_scatter(): return lax.psum_scatter(partial, 'dp', scatter_dimension=0, tiled=True)]
    dynamic_slice x8, local copies, waits for them, and re-layouts: 19.2 us -> 7.31 us  [chan_scatter(): mine = lax.dynamic_slice_in_dim(partial, (me ^ k) * width, width, 1)]
    dynamic_slice x0 -> x1, local copies, waits for them, and re-layouts: none -> 7.91 us  [body(): jnp.roll(val, (block_last - num // 2) * w_reduce.shape[1], axis=1)]
  transfers between devices with their start and end apart: 19 -> 25, of which waited for: 8 -> 11; matrix products, arithmetic and copies ran while one was open for 41% -> 30% of each run, Pallas kernels for 0% -> 0%
where the time goes in v1:
time: 787 us; the launch traced here: 776 us
  waiting for transfers between devices  386 us (49%)
  local copies, waits for them, and re-layouts  133 us (17%)
  matrix products  80.1 us (10%)
  starting transfers between devices  77.7 us (10%)
  other arithmetic  55.9 us (7%)
  blocking collectives  27.4 us (3%)
  between operations  16 us (2%)
    ppermute x4, waiting for transfers between devices, body(): x_next = lax.ppermute(local_out[-1], 'dp', perm=items)  158 us
    reduce_scatter x2, waiting for transfers between devices, dp_scatter(): return lax.psum_scatter(partial, 'dp', scatter_dimension=0, tiled=True)  157 us
    dynamic_update_slice x8, local copies, waits for them, and re-layouts, chan_gather(): whole = lax.dynamic_update_slice(whole, parts[k], (0, (me ^ k) * width))  64.4 us
    ppermute x6, waiting for transfers between devices, chan_scatter(): lax.ppermute(mine, 'chan', swap_pairs(k, n)).astype(jnp.float32)  28.4 us
    unnamed x215, local copies, waits for them, and re-layouts  27.3 us
    ppermute x4, starting transfers between devices, body(): x_next = lax.ppermute(local_out[-1], 'dp', perm=items)  25.6 us
    ppermute x3, starting transfers between devices, dp_total(): value = value + lax.ppermute(value, 'dp', swap_pairs(shift, n))  24.8 us
    ppermute x6, waiting for transfers between devices, chan_gather(): lax.ppermute(block, 'chan', swap_pairs(k, n))  16.7 us
  transfers between devices with their start and end apart: 25, of which 11 were waited for; matrix products, arithmetic and copies ran while one was open for 30% of the time, Pallas kernels for 0%

profile of v1, /device:TPU:0, one launch (start us, length us, event | category | flops | bytes accessed | tf_op | source)
XLA Modules:
  0.0 776.1 jit_solution(7831380215629716683)
XLA Ops:
  8.5 44.6 %collective-permute-done.6 = bf16[2816,352]{0,1:T(8,128)(2,1)S(1)} collective-permute-done((bf16[2816,352]{0,1:T(8,128)(2,1)}, bf16[2816,352]{0,1:T(8,128)(2,1)S(1)}, u32[]{:S(2)}, u32[]{:S(2)}) %collective-permute-start.6) | collective-permute-done | bytes 1982496 | tf_op jit(solution)/shard_map/ppermute | solution.py:96
  54.6 2.0 collective-permute-start.10
  58.6 3.0 collective-permute-start.3
  63.9 68.2 %collective-permute-done.7 = bf16[2816,352]{0,1:T(8,128)(2,1)} collective-permute-done((bf16[2816,352]{0,1:T(8,128)(2,1)S(1)}, bf16[2816,352]{0,1:T(8,128)(2,1)}, u32[]{:S(2)}, u32[]{:S(2)}) %collective-permute-start.7) | collective-permute-done | bytes 1982496 | tf_op jit(solution)/shard_map/ppermute | solution.py:96
  132.1 10.1 %collective-permute-start.8 = (bf16[2816,352]{0,1:T(8,128)(2,1)}, bf16[2816,352]{0,1:T(8,128)(2,1)}, u32[]{:S(2)}, u32[]{:S(2)}) collective-permute-start(bf16[2816,352]{0,1:T(8,128)(2,1)} %collective-permute-done.7), channel_id=1, source_target_pairs={{0,4},{4,8},{8,12},{12,16},{16,20},{20,24},{24,28},{28,0},{1,5},{5... | collective-permute-start | bytes 5947400 | tf_op jit(solution)/shard_map/ppermute | solution.py:96
  142.9 13.0 %fusion.108 = (f32[2,16,16]{2,1,0:T(8,128)S(1)}, f32[2,16,16,704]{3,2,1,0:T(8,128)S(1)}) fusion(f32[704]{0:T(1024)S(1)} %get-tuple-element.123, f32[704]{0:T(1024)S(1)} %get-tuple-element.124, f32[704]{0:T(1024)} %get-tuple-element.77, f32[704]{0:T(1024)} %get-tuple-element.78, f32[704]{0:T(1024)} %get-tuple-element.79, f32[704]{0:T(1024)} %get-tuple-element.80, ...), kind=kLoop, calls=%fused_computation.361 | loop fusion | flops 35323392 | bytes 3023616 | tf_op jit(solution)/shard_map/reduce_sum | solution.py:75
  156.3 8.9 %psum.28 = f32[512]{0:T(512)S(1)} all-reduce(f32[512]{0:T(512)S(1)} %reduce_sum.509), channel_id=1, replica_groups=mesh['dp'=8,'chan'=4] {'chan'}, use_global_device_ids=true, to_apply=%region_1.2 | all-reduce | flops 512 | bytes 4096 | tf_op jit(solution)/shard_map/psum | solution.py:75
  165.3 44.7 %collective-permute-done.8 = bf16[2816,352]{0,1:T(8,128)(2,1)} collective-permute-done((bf16[2816,352]{0,1:T(8,128)(2,1)}, bf16[2816,352]{0,1:T(8,128)(2,1)}, u32[]{:S(2)}, u32[]{:S(2)}) %collective-permute-start.8) | collective-permute-done | bytes 1982496 | tf_op jit(solution)/shard_map/ppermute | solution.py:96
  210.0 13.5 %collective-permute-start.9 = (bf16[2816,352]{0,1:T(8,128)(2,1)}, bf16[2816,352]{0,1:T(8,128)(2,1)}, u32[]{:S(2)}, u32[]{:S(2)}) collective-permute-start(bf16[2816,352]{0,1:T(8,128)(2,1)} %collective-permute-done.8), channel_id=1, source_target_pairs={{0,4},{4,8},{8,12},{12,16},{16,20},{20,24},{24,28},{28,0},{1,5},{5... | collective-permute-start | bytes 5947400 | tf_op jit(solution)/shard_map/ppermute | solution.py:96
  223.9 9.2 %psum.29 = f32[512]{0:T(512)S(1)} all-reduce(f32[512]{0:T(512)S(1)} %reduce_sum.511), channel_id=1, replica_groups=mesh['dp'=8,'chan'=4] {'chan'}, use_global_device_ids=true, to_apply=%region_3.4 | all-reduce | flops 512 | bytes 4096 | tf_op jit(solution)/shard_map/psum | solution.py:77
  236.1 16.7 %collective-permute-done.1 = bf16[512,704]{0,1:T(8,128)(2,1)S(1)} collective-permute-done((bf16[512,704]{0,1:T(8,128)(2,1)S(1)}, bf16[512,704]{0,1:T(8,128)(2,1)S(1)}, u32[]{:S(2)}, u32[]{:S(2)}) %collective-permute-start.1) | collective-permute-done | bytes 720928 | tf_op jit(solution)/shard_map/ppermute | solution.py:34
  253.0 2.6 collective-permute-start.5
  255.6 1.8 broadcast.39.clone
  257.4 7.8 dynamic_update_slice.24
  265.2 1.7 broadcast.39.clone.1
  266.9 7.8 %dynamic_update_slice.28 = bf16[512,2816]{1,0:T(8,128)(2,1)} dynamic-update-slice(bf16[512,2816]{1,0:T(8,128)(2,1)} %broadcast.39.clone.1, bf16[512,704]{1,0:T(8,128)(2,1)S(1)} %copy-done.12, s32[]{:T(128)} %constant.51.clone.1, s32[]{:T(128)S(6)} %select_n.21) | dynamic-update-slice | bytes 1441796 | tf_op jit(solution)/shard_map/dynamic_update_slice | solution.py:36
  276.1 8.6 %dynamic_update_slice.25 = bf16[512,2816]{1,0:T(8,128)(2,1)} dynamic-update-slice(bf16[512,2816]{1,0:T(8,128)(2,1)} %dynamic_update_slice.24, bf16[512,704]{1,0:T(8,128)(2,1)S(1)} %copy.17, s32[]{:T(128)} %constant.51.clone.1, s32[]{:T(128)S(6)} %select_n.38) | dynamic-update-slice | bytes 1441796 | tf_op jit(solution)/shard_map/dynamic_update_slice | solution.py:36
  286.1 8.7 %dynamic_update_slice.29 = bf16[512,2816]{1,0:T(8,128)(2,1)} dynamic-update-slice(bf16[512,2816]{1,0:T(8,128)(2,1)} %dynamic_update_slice.28, bf16[512,704]{1,0:T(8,128)(2,1)S(1)} %copy.23, s32[]{:T(128)} %constant.51.clone.1, s32[]{:T(128)S(6)} %select_n.38) | dynamic-update-slice | bytes 1441796 | tf_op jit(solution)/shard_map/dynamic_update_slice | solution.py:36
  295.1 7.7 dynamic_update_slice.26
  304.2 7.8 %dynamic_update_slice.30 = bf16[512,2816]{1,0:T(8,128)(2,1)} dynamic-update-slice(bf16[512,2816]{1,0:T(8,128)(2,1)} %dynamic_update_slice.29, bf16[512,704]{1,0:T(8,128)(2,1)S(1)} %copy.25, s32[]{:T(128)} %constant.51.clone.1, s32[]{:T(128)S(6)} %select_n.39) | dynamic-update-slice | bytes 1441796 | tf_op jit(solution)/shard_map/dynamic_update_slice | solution.py:36
  313.4 8.0 %dynamic_update_slice.27 = bf16[512,2816]{1,0:T(8,128)(2,1)} dynamic-update-slice(bf16[512,2816]{1,0:T(8,128)(2,1)} %dynamic_update_slice.26, bf16[512,704]{1,0:T(8,128)(2,1)S(1)} %copy.21, s32[]{:T(128)} %constant.51.clone.1, s32[]{:T(128)S(6)} %select_n.40) | dynamic-update-slice | bytes 1441796 | tf_op jit(solution)/shard_map/dynamic_update_slice | solution.py:36
  321.7 8.0 %dynamic_update_slice.31 = bf16[512,2816]{1,0:T(8,128)(2,1)} dynamic-update-slice(bf16[512,2816]{1,0:T(8,128)(2,1)} %dynamic_update_slice.30, bf16[512,704]{1,0:T(8,128)(2,1)S(1)} %copy.27, s32[]{:T(128)} %constant.51.clone.1, s32[]{:T(128)S(6)} %select_n.40) | dynamic-update-slice | bytes 1441796 | tf_op jit(solution)/shard_map/dynamic_update_slice | solution.py:36
  329.7 9.5 %collective-permute-start.12 = (bf16[2816,352]{0,1:T(8,128)(2,1)}, bf16[2816,352]{0,1:T(8,128)(2,1)S(1)}, u32[]{:S(2)}, u32[]{:S(2)}) collective-permute-start(bf16[2816,352]{0,1:T(8,128)(2,1)} %collective-permute-done.11), channel_id=1, source_target_pairs={{0,28},{4,0},{8,4},{12,8},{16,12},{20,16},{24,20},{28,24},{1,29},{... | collective-permute-start | bytes 5947400 | tf_op jit(solution)/shard_map/ppermute | solution.py:99
  340.9 1.7 constant_dynamic-update-slice_fusion.14
  342.6 1.8 constant_dynamic-update-slice_fusion.13
  344.9 1.7 constant_dynamic-update-slice_fusion.11
  346.5 1.7 constant_dynamic-update-slice_fusion.10
  348.2 1.7 constant_dynamic-update-slice_fusion.9
  349.9 11.9 %collective-permute-done.12 = bf16[2816,352]{0,1:T(8,128)(2,1)S(1)} collective-permute-done((bf16[2816,352]{0,1:T(8,128)(2,1)}, bf16[2816,352]{0,1:T(8,128)(2,1)S(1)}, u32[]{:S(2)}, u32[]{:S(2)}) %collective-permute-start.12) | collective-permute-done | bytes 1982496 | tf_op jit(solution)/shard_map/ppermute | solution.py:99
  362.0 1.7 constant_dynamic-update-slice_fusion.7
  363.7 1.7 constant_dynamic-update-slice_fusion.6
  365.3 1.7 constant_dynamic-update-slice_fusion.5
  367.2 1.7 constant_dynamic-update-slice_fusion.3
  368.8 1.7 constant_dynamic-update-slice_fusion.2
  370.5 1.7 constant_dynamic-update-slice_fusion.1
  372.4 7.9 %constant_dynamic-slice_fusion.6 = bf16[2816,2816]{0,1:T(8,128)(2,1)} fusion(bf16[2816,5632]{0,1:T(8,128)(2,1)S(1)} %constant_dynamic-update-slice_fusion, s32[]{:T(128)S(6)} %select_n.42), kind=kLoop, calls=%fused_computation.356 | loop fusion | bytes 31719428 | tf_op jit(solution)/shard_map/jit(_roll_dynamic)/dynamic_slice | solution.py:103
  380.3 15.3 %multiply_convert_fusion = (bf16[512,2816]{1,0:T(8,128)(2,1)S(1)}, f32[512,2816]{1,0:T(8,128)}) fusion(bf16[512,2816]{1,0:T(8,128)(2,1)} %dynamic_update_slice.27, bf16[2816,2816]{1,0:T(8,128)(2,1)} %all-gather.2.cloned.1.call-done), kind=kOutput, calls=%fused_computation.105 | convolution fusion | flops 8127381504 | bytes 27394048 | tf_op jit(solution)/shard_map/dot_general | solution.py:83
  397.1 11.9 %convolution_convert_fusion.1 = bf16[2816,2816]{1,0:T(8,128)(2,1)} fusion(bf16[512,2816]{1,0:T(8,128)(2,1)S(1)} %copy-done.15, bf16[512,2816]{1,0:T(8,128)(2,1)S(1)} %get-tuple-element.15), kind=kOutput, calls=%fused_computation.97 | convolution fusion | flops 8128102400 | bytes 21626880 | tf_op jit(solution)/shard_map/dot_general | solution.py:88
  409.3 14.4 %fusion.5 = bf16[512,2816]{1,0:T(8,128)(2,1)S(1)} fusion(f32[512,2816]{1,0:T(8,128)} %get-tuple-element.140, bf16[512,2816]{1,0:T(8,128)(2,1)S(1)} %copy-done.15, bf16[2816,2816]{0,1:T(8,128)(2,1)} %constant_dynamic-slice_fusion.6), kind=kOutput, calls=%fused_computation.104 | convolution fusion | flops 8134590464 | bytes 27394048 | tf_op jit(solution)/shard_map/dot_general | solution.py:106
  425.3 11.9 %convolution_convert_fusion = bf16[2816,2816]{1,0:T(8,128)(2,1)} fusion(bf16[512,2816]{1,0:T(8,128)(2,1)S(1)} %copy-done.16, bf16[512,2816]{1,0:T(8,128)(2,1)S(1)} %fusion.5), kind=kOutput, calls=%fused_computation.96 | convolution fusion | flops 8128102400 | bytes 21626880 | tf_op jit(solution)/shard_map/dot_general | solution.py:111
  437.3 1.8 copy-done.95
  439.1 13.0 %convolution_convert_fusion.3 = bf16[512,2816]{1,0:T(8,128)(2,1)S(1)} fusion(bf16[512,2816]{1,0:T(8,128)(2,1)S(1)} %copy-done.95, bf16[2816,2816]{0,1:T(8,128)(2,1)} %constant_dynamic-slice_fusion.6), kind=kOutput, calls=%fused_computation.108 | convolution fusion | flops 8121614336 | bytes 21626880 | tf_op jit(solution)/shard_map/dot_general | solution.py:122
  457.2 1.8 collective-permute-start.15
  459.7 13.5 %convolution_convert_fusion.2 = bf16[512,2816]{1,0:T(8,128)(2,1)S(1)} fusion(bf16[512,2816]{1,0:T(8,128)(2,1)} %copy-done.96, bf16[2816,2816]{1,0:T(8,128)(2,1)} %all-gather.2.cloned.1.call-done), kind=kOutput, calls=%fused_computation.107 | convolution fusion | flops 8121614336 | bytes 21626880 | tf_op jit(solution)/shard_map/dot_general | solution.py:118
  478.4 1.8 collective-permute-start.18
  480.9 2.3 copy.31
  483.1 2.3 copy.33
  485.4 2.3 copy.29
  487.7 28.4 %collective-permute-done.17 = bf16[512,704]{0,1:T(8,128)(2,1)S(1)} collective-permute-done((bf16[512,704]{0,1:T(8,128)(2,1)S(1)}, bf16[512,704]{0,1:T(8,128)(2,1)S(1)}, u32[]{:S(2)}, u32[]{:S(2)}) %collective-permute-start.17) | collective-permute-done | bytes 720928 | tf_op jit(solution)/shard_map/ppermute | solution.py:47
  518.5 2.3 copy.35
  520.8 5.8 fusion.105
  526.6 9.3 %all-reduce.2 = (f32[512]{0:T(512)S(1)}, f32[512]{0:T(512)S(1)}) all-reduce(f32[512]{0:T(512)S(1)} %get-tuple-element.143, f32[512]{0:T(512)S(1)} %get-tuple-element.142), channel_id=1, replica_groups=mesh['dp'=8,'chan'=4] {'chan'}, use_global_device_ids=true, to_apply=%region_7.8 | all-reduce | flops 1024 | bytes 8192 | tf_op jit(solution)/shard_map/psum | solution.py:130
  535.9 6.5 multiply_reduce_fusion.2
  542.7 4.1 multiply_reduce_fusion.1
  546.9 2.8 multiply_reduce_fusion.3
  551.0 4.5 collective-permute-start.19
  556.5 15.3 %collective-permute-start.20 = (f32[52,704]{1,0:T(8,128)S(1)}, f32[52,704]{1,0:T(8,128)S(1)}, u32[]{:S(2)}, u32[]{:S(2)}) collective-permute-start(f32[52,704]{1,0:T(8,128)S(1)} %fusion.121), channel_id=1, source_target_pairs={{0,8},{4,12},{8,0},{12,4},{16,24},{20,28},{24,16},{28,20},{1,9},{5... | collective-permute-start | bytes 439304 | tf_op jit(solution)/shard_map/ppermute | solution.py:59
  571.8 10.5 %collective-permute-done.20 = f32[52,704]{1,0:T(8,128)S(1)} collective-permute-done((f32[52,704]{1,0:T(8,128)S(1)}, f32[52,704]{1,0:T(8,128)S(1)}, u32[]{:S(2)}, u32[]{:S(2)}) %collective-permute-start.20) | collective-permute-done | bytes 146464 | tf_op jit(solution)/shard_map/ppermute | solution.py:59
  582.4 5.1 collective-permute-start.21
  587.8 13.3 %fusion.99 = bf16[2,16,16,704]{3,2,1,0:T(8,128)(2,1)} fusion(f32[2,16,16,704]{3,2,1,0:T(8,128)S(1)} %bitcast.104, bf16[2,16,16,704]{3,2,1,0:T(8,128)(2,1)S(1)} %copy-done.9, f32[704]{0:T(1024)S(1)} %copy-done.60, f32[704]{0:T(1024)S(1)} %copy-done.62, f32[704]{0:T(1024)S(1)} %copy-done.23, f32[704]{0:T(1024)S(1)} %copy-done.24, f32[704]{0:T(1024)S(1)} %copy-done.25, ...), kind=kLoop, calls=%fused_computation.203 | loop fusion | flops 36044800 | bytes 3021568 | tf_op jit(solution)/shard_map/convert_element_type | solution.py:158
  601.2 1.9 collective-permute-done.21
  605.2 3.7 convert_bitcast_fusion
  609.0 156.6 %reduce-scatter.3.cloned.1.call-done = bf16[352,2816]{1,0:T(8,128)(2,1)} async-done(((bf16[2816,2816]{1,0:T(8,128)(2,1)}), bf16[352,2816]{1,0:T(8,128)(2,1)}) %reduce-scatter.3.cloned.1.call-update) | async-done | bytes 1982480 | tf_op jit(solution)/shard_map/reduce_scatter | solution.py:52
  765.6 3.7 convert_element_type.89
  (336 shorter events, 41.3 us)
Async XLA Ops:
  7.2 49.5 %copy-start.8 = (bf16[2,16,16,704]{3,2,1,0:T(8,128)(2,1)S(1)}, bf16[2,16,16,704]{3,2,1,0:T(8,128)(2,1)}, u32[]{:S(2)}) copy-start(bf16[2,16,16,704]{3,2,1,0:T(8,128)(2,1)} %param.15) | copy-start | bytes 2162692
  7.2 373.1 %all-gather.2.cloned.1.call-start = ((), (), s32[]{:S(2)}) async-start(), calls=%async_computation.2 | async-start | bytes 17842176 | tf_op jit(solution)/shard_map/all_gather | solution.py:82
  7.9 597.3 %reduce-scatter.5.cloned.1.call-start = ((), (), s32[]{:S(2)}) async-start(), calls=%async_computation.4 | async-start | bytes 17842176 | tf_op jit(solution)/shard_map/reduce_scatter | solution.py:52
  8.0 45.1 %collective-permute-start.6 = (bf16[2816,352]{0,1:T(8,128)(2,1)}, bf16[2816,352]{0,1:T(8,128)(2,1)S(1)}, u32[]{:S(2)}, u32[]{:S(2)}) collective-permute-start(bf16[2816,352]{0,1:T(8,128)(2,1)} %param.13), channel_id=1, source_target_pairs={{0,4},{4,8},{8,12},{12,16},{16,20},{20,24},{24,28},{28,0},{1,5},{5... | collective-permute-start | bytes 5947400 | tf_op jit(solution)/shard_map/ppermute | solution.py:96
  53.1 79.0 %collective-permute-start.7 = (bf16[2816,352]{0,1:T(8,128)(2,1)S(1)}, bf16[2816,352]{0,1:T(8,128)(2,1)}, u32[]{:S(2)}, u32[]{:S(2)}) collective-permute-start(bf16[2816,352]{0,1:T(8,128)(2,1)S(1)} %collective-permute-done.6), channel_id=1, source_target_pairs={{0,4},{4,8},{8,12},{12,16},{16,20},{20,24},{24,28},{28,0},{1,5},{5... | collective-permute-start | bytes 5947400 | tf_op jit(solution)/shard_map/ppermute | solution.py:96
  54.6 110.7 %collective-permute-start.10 = (bf16[2816,352]{0,1:T(8,128)(2,1)}, bf16[2816,352]{0,1:T(8,128)(2,1)}, u32[]{:S(2)}, u32[]{:S(2)}) collective-permute-start(bf16[2816,352]{0,1:T(8,128)(2,1)} %param.13), channel_id=1, source_target_pairs={{0,28},{4,0},{8,4},{12,8},{16,12},{20,16},{24,20},{28,24},{1,29},{... | collective-permute-start | bytes 5947400 | tf_op jit(solution)/shard_map/ppermute | solution.py:99
  58.6 176.0 %collective-permute-start.3 = (bf16[512,704]{0,1:T(8,128)(2,1)}, bf16[512,704]{0,1:T(8,128)(2,1)}, u32[]{:S(2)}, u32[]{:S(2)}) collective-permute-start(bf16[512,704]{0,1:T(8,128)(2,1)} %copy.22), channel_id=1, source_target_pairs={{0,1},{1,0},{2,3},{3,2},{4,5},{5,4},{6,7},{7,6},{8,9},{9,8},{10,11... | collective-permute-start | bytes 2162696 | tf_op jit(solution)/shard_map/ppermute | solution.py:34
  63.0 92.9 %copy-start = (f32[2,16,16,704]{3,2,1,0:T(8,128)}, f32[2,16,16,704]{3,2,1,0:T(8,128)S(1)}, u32[]{:S(2)}) copy-start(f32[2,16,16,704]{3,2,1,0:T(8,128)S(1)} %convert_element_type.69) | copy-start | bytes 4325380
  132.1 77.9 %collective-permute-start.8 = (bf16[2816,352]{0,1:T(8,128)(2,1)}, bf16[2816,352]{0,1:T(8,128)(2,1)}, u32[]{:S(2)}, u32[]{:S(2)}) collective-permute-start(bf16[2816,352]{0,1:T(8,128)(2,1)} %collective-permute-done.7), channel_id=1, source_target_pairs={{0,4},{4,8},{8,12},{12,16},{16,20},{20,24},{24,28},{28,0},{1,5},{5... | collective-permute-start | bytes 5947400 | tf_op jit(solution)/shard_map/ppermute | solution.py:96
  156.2 77.2 %copy-start.2 = (f32[2,16,16,704]{3,2,1,0:T(8,128)}, f32[2,16,16,704]{3,2,1,0:T(8,128)S(1)}, u32[]{:S(2)}) copy-start(f32[2,16,16,704]{3,2,1,0:T(8,128)S(1)} %get-tuple-element.130) | copy-start | bytes 4325380
  156.2 76.9 %copy-start.20 = (f32[704]{0:T(1024)S(1)}, f32[704]{0:T(1024)}, u32[]{:S(2)}) copy-start(f32[704]{0:T(1024)} %param.10) | copy-start | bytes 8452
  156.2 76.9 %copy-start.93 = (f32[704]{0:T(1024)S(1)}, f32[704]{0:T(1024)}, u32[]{:S(2)}) copy-start(f32[704]{0:T(1024)} %param.11) | copy-start | bytes 8452
  165.2 67.9 %copy-start.18 = (f32[512]{0:T(512)}, f32[512]{0:T(512)S(1)}, u32[]{:S(2)}) copy-start(f32[512]{0:T(512)S(1)} %broadcast_multiply_fusion.2) | copy-start | bytes 6148
  165.3 164.4 %collective-permute-start.11 = (bf16[2816,352]{0,1:T(8,128)(2,1)}, bf16[2816,352]{0,1:T(8,128)(2,1)}, u32[]{:S(2)}, u32[]{:S(2)}) collective-permute-start(bf16[2816,352]{0,1:T(8,128)(2,1)} %collective-permute-done.10), channel_id=1, source_target_pairs={{0,28},{4,0},{8,4},{12,8},{16,12},{20,16},{24,20},{28,24},{1,29},{... | collective-permute-start | bytes 5947400 | tf_op jit(solution)/shard_map/ppermute | solution.py:99
  210.0 129.2 %collective-permute-start.9 = (bf16[2816,352]{0,1:T(8,128)(2,1)}, bf16[2816,352]{0,1:T(8,128)(2,1)}, u32[]{:S(2)}, u32[]{:S(2)}) collective-permute-start(bf16[2816,352]{0,1:T(8,128)(2,1)} %collective-permute-done.8), channel_id=1, source_target_pairs={{0,4},{4,8},{8,12},{12,16},{16,20},{20,24},{24,28},{28,0},{1,5},{5... | collective-permute-start | bytes 5947400 | tf_op jit(solution)/shard_map/ppermute | solution.py:96
  233.7 19.0 %collective-permute-start.1 = (bf16[512,704]{0,1:T(8,128)(2,1)S(1)}, bf16[512,704]{0,1:T(8,128)(2,1)S(1)}, u32[]{:S(2)}, u32[]{:S(2)}) collective-permute-start(bf16[512,704]{0,1:T(8,128)(2,1)S(1)} %copy.16), channel_id=1, source_target_pairs={{0,2},{1,3},{2,0},{3,1},{4,6},{5,7},{6,4},{7,5},{8,10},{9,11},{10,... | collective-permute-start | bytes 2162696 | tf_op jit(solution)/shard_map/ppermute | solution.py:34
  234.3 18.7 %collective-permute-start = (bf16[512,704]{0,1:T(8,128)(2,1)S(1)}, bf16[512,704]{0,1:T(8,128)(2,1)}, u32[]{:S(2)}, u32[]{:S(2)}) collective-permute-start(bf16[512,704]{0,1:T(8,128)(2,1)S(1)} %copy.16), channel_id=1, source_target_pairs={{0,1},{1,0},{2,3},{3,2},{4,5},{5,4},{6,7},{7,6},{8,9},{9,8},{10,11... | collective-permute-start | bytes 2162696 | tf_op jit(solution)/shard_map/ppermute | solution.py:34
  234.6 68.2 %collective-permute-start.4 = (bf16[512,704]{0,1:T(8,128)(2,1)}, bf16[512,704]{0,1:T(8,128)(2,1)}, u32[]{:S(2)}, u32[]{:S(2)}) collective-permute-start(bf16[512,704]{0,1:T(8,128)(2,1)} %copy.22), channel_id=1, source_target_pairs={{0,2},{1,3},{2,0},{3,1},{4,6},{5,7},{6,4},{7,5},{8,10},{9,11},{10,... | collective-permute-start | bytes 2162696 | tf_op jit(solution)/shard_map/ppermute | solution.py:34
  252.7 59.3 %collective-permute-start.2 = (bf16[512,704]{0,1:T(8,128)(2,1)S(1)}, bf16[512,704]{0,1:T(8,128)(2,1)}, u32[]{:S(2)}, u32[]{:S(2)}) collective-permute-start(bf16[512,704]{0,1:T(8,128)(2,1)S(1)} %copy.16), channel_id=1, source_target_pairs={{0,3},{1,2},{2,1},{3,0},{4,7},{5,6},{6,5},{7,4},{8,11},{9,10},{10,... | collective-permute-start | bytes 2162696 | tf_op jit(solution)/shard_map/ppermute | solution.py:34
  253.0 68.4 %collective-permute-start.5 = (bf16[512,704]{0,1:T(8,128)(2,1)}, bf16[512,704]{0,1:T(8,128)(2,1)S(1)}, u32[]{:S(2)}, u32[]{:S(2)}) collective-permute-start(bf16[512,704]{0,1:T(8,128)(2,1)} %copy.22), channel_id=1, source_target_pairs={{0,3},{1,2},{2,1},{3,0},{4,7},{5,6},{6,5},{7,4},{8,11},{9,10},{10,... | collective-permute-start | bytes 2162696 | tf_op jit(solution)/shard_map/ppermute | solution.py:34
  329.7 32.2 %collective-permute-start.12 = (bf16[2816,352]{0,1:T(8,128)(2,1)}, bf16[2816,352]{0,1:T(8,128)(2,1)S(1)}, u32[]{:S(2)}, u32[]{:S(2)}) collective-permute-start(bf16[2816,352]{0,1:T(8,128)(2,1)} %collective-permute-done.11), channel_id=1, source_target_pairs={{0,28},{4,0},{8,4},{12,8},{16,12},{20,16},{24,20},{28,24},{1,29},{... | collective-permute-start | bytes 5947400 | tf_op jit(solution)/shard_map/ppermute | solution.py:99
  409.1 356.6 %reduce-scatter.3.cloned.1.call-start = ((), (), s32[]{:S(2)}) async-start(), calls=%async_computation.3 | async-start | bytes 17842176 | tf_op jit(solution)/shard_map/reduce_scatter | solution.py:52
  456.2 24.0 %collective-permute-start.14 = (bf16[512,704]{0,1:T(8,128)(2,1)}, bf16[512,704]{0,1:T(8,128)(2,1)}, u32[]{:S(2)}, u32[]{:S(2)}) collective-permute-start(bf16[512,704]{0,1:T(8,128)(2,1)} %copy.30), channel_id=1, source_target_pairs={{0,2},{1,3},{2,0},{3,1},{4,6},{5,7},{6,4},{7,5},{8,10},{9,11},{10,... | collective-permute-start | bytes 2162696 | tf_op jit(solution)/shard_map/ppermute | solution.py:47
  457.2 26.0 %collective-permute-start.15 = (bf16[512,704]{0,1:T(8,128)(2,1)}, bf16[512,704]{0,1:T(8,128)(2,1)}, u32[]{:S(2)}, u32[]{:S(2)}) collective-permute-start(bf16[512,704]{0,1:T(8,128)(2,1)} %copy.32), channel_id=1, source_target_pairs={{0,3},{1,2},{2,1},{3,0},{4,7},{5,6},{6,5},{7,4},{8,11},{9,10},{10,... | collective-permute-start | bytes 2162696 | tf_op jit(solution)/shard_map/ppermute | solution.py:47
  459.0 26.4 %collective-permute-start.13 = (bf16[512,704]{0,1:T(8,128)(2,1)S(1)}, bf16[512,704]{0,1:T(8,128)(2,1)}, u32[]{:S(2)}, u32[]{:S(2)}) collective-permute-start(bf16[512,704]{0,1:T(8,128)(2,1)S(1)} %copy.28), channel_id=1, source_target_pairs={{0,1},{1,0},{2,3},{3,2},{4,5},{5,4},{6,7},{7,6},{8,9},{9,8},{10,11... | collective-permute-start | bytes 2162696 | tf_op jit(solution)/shard_map/ppermute | solution.py:47
  476.2 40.0 %collective-permute-start.17 = (bf16[512,704]{0,1:T(8,128)(2,1)S(1)}, bf16[512,704]{0,1:T(8,128)(2,1)S(1)}, u32[]{:S(2)}, u32[]{:S(2)}) collective-permute-start(bf16[512,704]{0,1:T(8,128)(2,1)S(1)} %copy.36), channel_id=1, source_target_pairs={{0,2},{1,3},{2,0},{3,1},{4,6},{5,7},{6,4},{7,5},{8,10},{9,11},{10,... | collective-permute-start | bytes 2162696 | tf_op jit(solution)/shard_map/ppermute | solution.py:47
  478.4 38.9 %collective-permute-start.18 = (bf16[512,704]{0,1:T(8,128)(2,1)}, bf16[512,704]{0,1:T(8,128)(2,1)S(1)}, u32[]{:S(2)}, u32[]{:S(2)}) collective-permute-start(bf16[512,704]{0,1:T(8,128)(2,1)} %copy.38), channel_id=1, source_target_pairs={{0,3},{1,2},{2,1},{3,0},{4,7},{5,6},{6,5},{7,4},{8,11},{9,10},{10,... | collective-permute-start | bytes 2162696 | tf_op jit(solution)/shard_map/ppermute | solution.py:47
  480.2 38.3 %collective-permute-start.16 = (bf16[512,704]{0,1:T(8,128)(2,1)}, bf16[512,704]{0,1:T(8,128)(2,1)}, u32[]{:S(2)}, u32[]{:S(2)}) collective-permute-start(bf16[512,704]{0,1:T(8,128)(2,1)} %copy.34), channel_id=1, source_target_pairs={{0,1},{1,0},{2,3},{3,2},{4,5},{5,4},{6,7},{7,6},{8,9},{9,8},{10,11... | collective-permute-start | bytes 2162696 | tf_op jit(solution)/shard_map/ppermute | solution.py:47
  549.7 37.7 %copy-start.5 = (f32[512,704]{1,0:T(8,128)S(1)}, f32[512,704]{1,0:T(8,128)}, u32[]{:S(2)}) copy-start(f32[512,704]{1,0:T(8,128)} %copy-done.4) | copy-start | bytes 4325380
  549.7 37.7 %copy-start.9 = (bf16[2,16,16,704]{3,2,1,0:T(8,128)(2,1)S(1)}, bf16[2,16,16,704]{3,2,1,0:T(8,128)(2,1)}, u32[]{:S(2)}) copy-start(bf16[2,16,16,704]{3,2,1,0:T(8,128)(2,1)} %param.15) | copy-start | bytes 2162692
  549.7 37.7 %copy-start.22 = (f32[704]{0:T(1024)S(1)}, f32[704]{0:T(1024)}, u32[]{:S(2)}) copy-start(f32[704]{0:T(1024)} %get-tuple-element.76) | copy-start | bytes 8452
  549.8 37.7 %copy-start.23 = (f32[704]{0:T(1024)S(1)}, f32[704]{0:T(1024)}, u32[]{:S(2)}) copy-start(f32[704]{0:T(1024)} %get-tuple-element.77) | copy-start | bytes 8452
  549.8 37.7 %copy-start.24 = (f32[704]{0:T(1024)S(1)}, f32[704]{0:T(1024)}, u32[]{:S(2)}) copy-start(f32[704]{0:T(1024)} %get-tuple-element.78) | copy-start | bytes 8452
  549.8 37.7 %copy-start.25 = (f32[704]{0:T(1024)S(1)}, f32[704]{0:T(1024)}, u32[]{:S(2)}) copy-start(f32[704]{0:T(1024)} %get-tuple-element.79) | copy-start | bytes 8452
  549.8 37.7 %copy-start.26 = (f32[704]{0:T(1024)S(1)}, f32[704]{0:T(1024)}, u32[]{:S(2)}) copy-start(f32[704]{0:T(1024)} %get-tuple-element.80) | copy-start | bytes 8452
  549.8 37.7 %copy-start.27 = (f32[704]{0:T(1024)S(1)}, f32[704]{0:T(1024)}, u32[]{:S(2)}) copy-start(f32[704]{0:T(1024)} %get-tuple-element.81) | copy-start | bytes 8452
  549.8 37.7 %copy-start.28 = (f32[704]{0:T(1024)S(1)}, f32[704]{0:T(1024)}, u32[]{:S(2)}) copy-start(f32[704]{0:T(1024)} %get-tuple-element.82) | copy-start | bytes 8452
  549.8 37.7 %copy-start.29 = (f32[704]{0:T(1024)S(1)}, f32[704]{0:T(1024)}, u32[]{:S(2)}) copy-start(f32[704]{0:T(1024)} %get-tuple-element.83) | copy-start | bytes 8452
  549.8 37.7 %copy-start.30 = (f32[704]{0:T(1024)S(1)}, f32[704]{0:T(1024)}, u32[]{:S(2)}) copy-start(f32[704]{0:T(1024)} %get-tuple-element.84) | copy-start | bytes 8452
  549.8 37.7 %copy-start.31 = (f32[704]{0:T(1024)S(1)}, f32[704]{0:T(1024)}, u32[]{:S(2)}) copy-start(f32[704]{0:T(1024)} %get-tuple-element.85) | copy-start | bytes 8452
  549.9 37.7 %copy-start.32 = (f32[704]{0:T(1024)S(1)}, f32[704]{0:T(1024)}, u32[]{:S(2)}) copy-start(f32[704]{0:T(1024)} %get-tuple-element.86) | copy-start | bytes 8452
  549.9 37.7 %copy-start.33 = (f32[704]{0:T(1024)S(1)}, f32[704]{0:T(1024)}, u32[]{:S(2)}) copy-start(f32[704]{0:T(1024)} %get-tuple-element.87) | copy-start | bytes 8452
  549.9 37.7 %copy-start.34 = (f32[704]{0:T(1024)S(1)}, f32[704]{0:T(1024)}, u32[]{:S(2)}) copy-start(f32[704]{0:T(1024)} %get-tuple-element.88) | copy-start | bytes 8452
  549.9 37.7 %copy-start.35 = (f32[704]{0:T(1024)S(1)}, f32[704]{0:T(1024)}, u32[]{:S(2)}) copy-start(f32[704]{0:T(1024)} %get-tuple-element.89) | copy-start | bytes 8452
  549.9 37.7 %copy-start.36 = (f32[704]{0:T(1024)S(1)}, f32[704]{0:T(1024)}, u32[]{:S(2)}) copy-start(f32[704]{0:T(1024)} %get-tuple-element.90) | copy-start | bytes 8452
  549.9 37.7 %copy-start.37 = (f32[704]{0:T(1024)S(1)}, f32[704]{0:T(1024)}, u32[]{:S(2)}) copy-start(f32[704]{0:T(1024)} %get-tuple-element.91) | copy-start | bytes 8452
  549.9 37.7 %copy-start.38 = (f32[704]{0:T(1024)S(1)}, f32[704]{0:T(1024)}, u32[]{:S(2)}) copy-start(f32[704]{0:T(1024)} %get-tuple-element.92) | copy-start | bytes 8452
  549.9 37.7 %copy-start.39 = (f32[704]{0:T(1024)S(1)}, f32[704]{0:T(1024)}, u32[]{:S(2)}) copy-start(f32[704]{0:T(1024)} %get-tuple-element.93) | copy-start | bytes 8452
  549.9 37.7 %copy-start.40 = (f32[704]{0:T(1024)S(1)}, f32[704]{0:T(1024)}, u32[]{:S(2)}) copy-start(f32[704]{0:T(1024)} %get-tuple-element.94) | copy-start | bytes 8452
  549.9 37.7 %copy-start.42 = (f32[704]{0:T(1024)S(1)}, f32[704]{0:T(1024)}, u32[]{:S(2)}) copy-start(f32[704]{0:T(1024)} %copy-done.41) | copy-start | bytes 8452
  550.0 37.7 %copy-start.44 = (f32[704]{0:T(1024)S(1)}, f32[704]{0:T(1024)}, u32[]{:S(2)}) copy-start(f32[704]{0:T(1024)} %copy-done.43) | copy-start | bytes 8452
  550.0 37.7 %copy-start.46 = (f32[704]{0:T(1024)S(1)}, f32[704]{0:T(1024)}, u32[]{:S(2)}) copy-start(f32[704]{0:T(1024)} %copy-done.45) | copy-start | bytes 8452
  550.0 37.7 %copy-start.48 = (f32[704]{0:T(1024)S(1)}, f32[704]{0:T(1024)}, u32[]{:S(2)}) copy-start(f32[704]{0:T(1024)} %copy-done.47) | copy-start | bytes 8452
  550.0 37.7 %copy-start.50 = (f32[704]{0:T(1024)S(1)}, f32[704]{0:T(1024)}, u32[]{:S(2)}) copy-start(f32[704]{0:T(1024)} %copy-done.49) | copy-start | bytes 8452
  550.0 37.7 %copy-start.52 = (f32[704]{0:T(1024)S(1)}, f32[704]{0:T(1024)}, u32[]{:S(2)}) copy-start(f32[704]{0:T(1024)} %copy-done.51) | copy-start | bytes 8452
  550.0 37.7 %copy-start.54 = (f32[704]{0:T(1024)S(1)}, f32[704]{0:T(1024)}, u32[]{:S(2)}) copy-start(f32[704]{0:T(1024)} %copy-done.53) | copy-start | bytes 8452
  550.0 37.7 %copy-start.56 = (f32[704]{0:T(1024)S(1)}, f32[704]{0:T(1024)}, u32[]{:S(2)}) copy-start(f32[704]{0:T(1024)} %copy-done.55) | copy-start | bytes 8452
  550.0 37.7 %copy-start.58 = (f32[704]{0:T(1024)S(1)}, f32[704]{0:T(1024)}, u32[]{:S(2)}) copy-start(f32[704]{0:T(1024)} %copy-done.57) | copy-start | bytes 8452
  550.0 37.7 %copy-start.60 = (f32[704]{0:T(1024)S(1)}, f32[704]{0:T(1024)}, u32[]{:S(2)}) copy-start(f32[704]{0:T(1024)} %copy-done.59) | copy-start | bytes 8452
  550.0 37.7 %copy-start.62 = (f32[704]{0:T(1024)S(1)}, f32[704]{0:T(1024)}, u32[]{:S(2)}) copy-start(f32[704]{0:T(1024)} %copy-done.61) | copy-start | bytes 8452
  550.1 37.7 %copy-start.64 = (f32[704]{0:T(1024)S(1)}, f32[704]{0:T(1024)}, u32[]{:S(2)}) copy-start(f32[704]{0:T(1024)} %copy-done.63) | copy-start | bytes 8452
  551.0 5.5 collective-permute-start.19
  556.5 25.8 %collective-permute-start.20 = (f32[52,704]{1,0:T(8,128)S(1)}, f32[52,704]{1,0:T(8,128)S(1)}, u32[]{:S(2)}, u32[]{:S(2)}) collective-permute-start(f32[52,704]{1,0:T(8,128)S(1)} %fusion.121), channel_id=1, source_target_pairs={{0,8},{4,12},{8,0},{12,4},{16,24},{20,28},{24,16},{28,20},{1,9},{5... | collective-permute-start | bytes 439304 | tf_op jit(solution)/shard_map/ppermute | solution.py:59
  582.4 20.7 %collective-permute-start.21 = (f32[52,704]{1,0:T(8,128)S(1)}, f32[52,704]{1,0:T(8,128)S(1)}, u32[]{:S(2)}, u32[]{:S(2)}) collective-permute-start(f32[52,704]{1,0:T(8,128)S(1)} %add.511), channel_id=1, source_target_pairs={{0,16},{4,20},{8,24},{12,28},{16,0},{20,4},{24,8},{28,12},{1,17},{... | collective-permute-start | bytes 439304 | tf_op jit(solution)/shard_map/ppermute | solution.py:59
  (58 other events, 756.7 us)
Sparse Core Ops, SparseCore 0:
  9.7 242.2 all-gather.1
  409.2 196.0 reduce-scatter.4
  607.6 157.9 reduce-scatter.2
